TPU v7x, 32 devices: a whole 2x2x4 slice. The times are simulated.
32 devices in a mesh: dp: 8 (over y, x, core), section: 4 (over z).
Axes of the slice: x: 2, y: 2, z: 4, core: 2. Of those that a mesh axis runs over, the one named last changes fastest.
Arguments:
- acts: bfloat16 [8, 4, 2, 64, 4096], P('dp', 'section'), may hold values from -6 to 6
- weight_v: bfloat16 [4, 4096, 512], P('section'), may hold values from -0.09375 to 0.09375
- weight_o: bfloat16 [4, 512, 4096], P('section'), may hold values from -0.09375 to 0.09375
- top_grad: bfloat16 [8, 2, 64, 4096], P('dp'), may hold values from -6 to 6
- loss_mask: int32 [8, 2, 64], P('dp'), may hold values 0 or 1
- q_prev: float32 [4, 512, 64], P('section'), may hold values from -0.25 to 0.25
Outputs:
- basis: float32 [4, 4096, 64], P('section')
- q_next: float32 [4, 512, 64], P('section')
All inputs are finite; a program needn't handle non-finite values. No bound on the sum of `loss_mask` on one device may be relied on, other than what follows from the above.
Results may differ from a plain program's by a relative error of at most 0.01.
Values may be sent and summed in bfloat16 or wider, within the bound.
A program may use at most 128 MiB of HBM per device.

v0:
```python
import math

import jax
import jax.numpy as jnp
from jax import lax
from jax.sharding import PartitionSpec as P


def passed_along(value, axis, steps):
    count = lax.axis_size(axis)
    initial, last = (max(0, -steps), min(count, count - steps))
    return lax.ppermute(value, axis, [(source, source + steps) for source in range(initial, last)])


def propagate(w_value, w_output, grad_in):
    dvalue = jnp.einsum("td,vd->tv", grad_in, w_output, preferred_element_type=jnp.float32).astype(
        jnp.bfloat16
    )
    passed = (
        grad_in.astype(jnp.float32)
        + jnp.einsum("tv,dv->td", dvalue, w_value, preferred_element_type=jnp.float32)
    ).astype(jnp.bfloat16)
    return (passed, dvalue)


def local(acts, weight_v, weight_o, top_grad, loss_mask, q_prev):
    high = lax.Precision.HIGHEST
    inputs = acts[0, 0]
    w_value = weight_v[0]
    w_output = weight_o[0]
    right = q_prev[0]
    batches, tokens, width = inputs.shape
    features = w_value.shape[1]
    sections = lax.axis_size("section")
    here = lax.axis_index("section")
    at_end = here == sections - 1
    seed = (top_grad[0].astype(jnp.float32) * loss_mask[0][..., None].astype(jnp.float32)).astype(
        jnp.bfloat16
    )
    kept_v = jnp.zeros((batches, tokens, features), jnp.bfloat16)

    def advance(step, carry):
        incoming, kept_d = carry
        batch = step - (sections - 1 - here)
        safe = jnp.clip(batch, 0, batches - 1)
        grad_in = jnp.where(at_end, lax.dynamic_index_in_dim(seed, safe, 0, False), incoming)

        def work(operand):
            passed, dvalue = propagate(w_value, w_output, operand)
            return (passed, lax.dynamic_update_index_in_dim(kept_d, dvalue, safe, 0))

        def rest(operand):
            return (jnp.zeros_like(operand), kept_d)

        active = jnp.logical_and(batch >= 0, batch < batches)
        passed, kept_d = lax.cond(active, work, rest, grad_in)
        incoming = passed_along(passed, "section", -1)
        return (incoming, kept_d)

    start = (jnp.zeros((tokens, width), jnp.bfloat16), kept_v)
    _, kept_d = lax.fori_loop(0, sections + batches - 1, advance, start)
    rows = inputs.reshape(-1, width)
    dvalue = kept_d.reshape(-1, features)
    replicas = lax.axis_size("dp")
    gradient = jnp.einsum("td,tv->dv", rows, dvalue, preferred_element_type=jnp.float32)
    term_left = jnp.dot(gradient, right, precision=high)
    left = lax.psum(term_left, "dp") / replicas
    gram = jnp.dot(left.T, left, precision=high)
    lower = jnp.linalg.cholesky(gram)
    unit = lax.linalg.triangular_solve(lower, left, left_side=False, lower=True, transpose_a=True)
    term_right = jnp.einsum("dv,dr->vr", gradient, unit, precision=high)
    fresh = lax.psum(term_right, "dp") / replicas
    return ((unit * math.sqrt(width))[None], fresh[None])


def solution(mesh):
    placed = (
        P("dp", "section", None, None, None),
        P("section", None, None),
        P("section", None, None),
        P("dp", None, None, None),
        P("dp", None, None),
        P("section", None, None),
    )
    return jax.shard_map(
        local,
        mesh=mesh,
        in_specs=placed,
        out_specs=(P("section", None, None), P("section", None, None)),
        check_vma=False,
    )
```

profile of v0, /device:TPU:0, one launch (start us, length us, event | category | flops | bytes accessed | tf_op | source)
XLA Modules:
  0.0 263.2 jit_solution(11875892096922863952)
XLA Ops:
  7.2 0.0 copy-start
  7.2 0.0 all-reduce.3.cloned.1.call-start
  7.2 0.8 convert_bitcast_fusion
  8.0 1.5 fusion.2
  9.5 97.9 %while.20 = (s32[]{:T(128)}, bf16[64,4096]{1,0:T(8,128)(2,1)S(1)}, bf16[2,64,512]{2,1,0:T(8,128)(2,1)S(1)}, s32[]{:T(128)}, pred[]{:T(512)}, /*index=5*/bf16[2,6...) while((s32[]{:T(128)}, bf16[64,4096]{1,0:T(8,128)(2,1)S(1)}, ...), condition=%wide.region_3.4_spmd, body=%wide.region_0.3_spmd.sunk | while | flops 538214400 | bytes 30082364 | solution.py:61
  9.6 0.1 conditional.2
  9.6 1.3 collective-permute-start
  10.9 15.6 %collective-permute-done = bf16[64,4096]{1,0:T(8,128)(2,1)S(1)} collective-permute-done((bf16[64,4096]{1,0:T(8,128)(2,1)S(1)}, bf16[64,4096]{1,0:T(8,128)(2,1)S(1)}, u32[]{:S(2)}, u32[]{:S(2)}) %collective-permute-start) | collective-permute-done | bytes 524320 | tf_op jit(solution)/shard_map/while/body/eval_jaxpr/ppermute | solution.py:12
  26.6 1.3 collective-permute-start
  27.9 13.7 %collective-permute-done = bf16[64,4096]{1,0:T(8,128)(2,1)S(1)} collective-permute-done((bf16[64,4096]{1,0:T(8,128)(2,1)S(1)}, bf16[64,4096]{1,0:T(8,128)(2,1)S(1)}, u32[]{:S(2)}, u32[]{:S(2)}) %collective-permute-start) | collective-permute-done | bytes 524320 | tf_op jit(solution)/shard_map/while/body/eval_jaxpr/ppermute | solution.py:12
  41.6 1.3 collective-permute-start
  42.9 27.4 %collective-permute-done = bf16[64,4096]{1,0:T(8,128)(2,1)S(1)} collective-permute-done((bf16[64,4096]{1,0:T(8,128)(2,1)S(1)}, bf16[64,4096]{1,0:T(8,128)(2,1)S(1)}, u32[]{:S(2)}, u32[]{:S(2)}) %collective-permute-start) | collective-permute-done | bytes 524320 | tf_op jit(solution)/shard_map/while/body/eval_jaxpr/ppermute | solution.py:12
  70.3 5.1 %conditional.2 = (bf16[64,4096]{1,0:T(8,128)(2,1)S(1)}, bf16[2,64,512]{2,1,0:T(8,128)(2,1)S(1)}) conditional(s32[]{:T(128)} %convert_element_type.56, bf16[2,64,512]{2,1,0:T(8,128)(2,1)S(1)} %get-tuple-element.351, (pred[]{:T(512)}, s32[]{:T(128)}, bf16[2,64,4096]{2,1,0:T(8,128)(2,1)S(1)}, bf16[64,4096]{1,0:T(8,128)(2,1)S(1)}, ...), branch_computations={%region_1.1_spmd, %region_2.2_spmd} | conditional | flops 538214400 | bytes 27984968 | solution.py:56
  70.3 0.0 copy-start.1
  70.3 3.7 %bitcast_dynamic-update-slice_fusion = (bf16[2,64,512]{2,1,0:T(8,128)(2,1)S(1)}, bf16[64,512]{1,0:T(8,128)(2,1)S(1)}) fusion(bf16[2,64,512]{2,1,0:T(8,128)(2,1)S(1)} %get-tuple-element.247, s32[]{:T(128)S(6)} %min.10, bf16[512,4096]{1,0:T(8,128)(2,1)} %get-tuple-element.245, bf16[64,4096]{1,0:T(8,128)(2,1)S(1)} %get-tuple-element.244, ...), kind=kOutput, calls=%fused_computation.4 | convolution fusion | flops 268730368 | bytes 5374977 | tf_op jit(solution)/shard_map/while/body/eval_jaxpr/cond/branch_1_fun/td,vd->tv/dot_general | solution.py:16
  74.1 0.0 copy-done.1
  74.1 1.4 fusion
  75.5 1.3 collective-permute-start
  76.8 12.5 %collective-permute-done = bf16[64,4096]{1,0:T(8,128)(2,1)S(1)} collective-permute-done((bf16[64,4096]{1,0:T(8,128)(2,1)S(1)}, bf16[64,4096]{1,0:T(8,128)(2,1)S(1)}, u32[]{:S(2)}, u32[]{:S(2)}) %collective-permute-start) | collective-permute-done | bytes 524320 | tf_op jit(solution)/shard_map/while/body/eval_jaxpr/ppermute | solution.py:12
  89.3 5.1 %conditional.2 = (bf16[64,4096]{1,0:T(8,128)(2,1)S(1)}, bf16[2,64,512]{2,1,0:T(8,128)(2,1)S(1)}) conditional(s32[]{:T(128)} %convert_element_type.56, bf16[2,64,512]{2,1,0:T(8,128)(2,1)S(1)} %get-tuple-element.351, (pred[]{:T(512)}, s32[]{:T(128)}, bf16[2,64,4096]{2,1,0:T(8,128)(2,1)S(1)}, bf16[64,4096]{1,0:T(8,128)(2,1)S(1)}, ...), branch_computations={%region_1.1_spmd, %region_2.2_spmd} | conditional | flops 538214400 | bytes 27984968 | solution.py:56
  89.3 0.0 copy-start.1
  89.3 3.7 %bitcast_dynamic-update-slice_fusion = (bf16[2,64,512]{2,1,0:T(8,128)(2,1)S(1)}, bf16[64,512]{1,0:T(8,128)(2,1)S(1)}) fusion(bf16[2,64,512]{2,1,0:T(8,128)(2,1)S(1)} %get-tuple-element.247, s32[]{:T(128)S(6)} %min.10, bf16[512,4096]{1,0:T(8,128)(2,1)} %get-tuple-element.245, bf16[64,4096]{1,0:T(8,128)(2,1)S(1)} %get-tuple-element.244, ...), kind=kOutput, calls=%fused_computation.4 | convolution fusion | flops 268730368 | bytes 5374977 | tf_op jit(solution)/shard_map/while/body/eval_jaxpr/cond/branch_1_fun/td,vd->tv/dot_general | solution.py:16
  93.0 0.0 copy-done.1
  93.0 1.4 fusion
  94.4 1.3 collective-permute-start
  95.7 11.7 %collective-permute-done = bf16[64,4096]{1,0:T(8,128)(2,1)S(1)} collective-permute-done((bf16[64,4096]{1,0:T(8,128)(2,1)S(1)}, bf16[64,4096]{1,0:T(8,128)(2,1)S(1)}, u32[]{:S(2)}, u32[]{:S(2)}) %collective-permute-start) | collective-permute-done | bytes 524320 | tf_op jit(solution)/shard_map/while/body/eval_jaxpr/ppermute | solution.py:12
  107.4 0.0 copy-done
  107.4 0.0 copy-start.3
  107.4 1.3 fusion.16
  108.7 0.0 copy-start.2
  108.7 3.2 %copy-done.2 = f32[512,4096]{1,0:T(8,128)} copy-done((f32[512,4096]{1,0:T(8,128)}, f32[512,4096]{1,0:T(8,128)S(1)}, u32[]{:S(2)}) %copy-start.2) | copy-done | bytes 8388632
  111.9 0.0 copy-done.3
  111.9 6.6 %fusion.9 = f32[4096,64]{0,1:T(8,128)} fusion(f32[512,4096]{1,0:T(8,128)S(1)} %fusion.16, f32[1,512,64]{1,2,0:T(8,128)S(1)} %copy-done.3), kind=kOutput, calls=%fused_computation.15 | convolution fusion | flops 1610612736 | bytes 9568256 | tf_op jit(solution)/shard_map/dot_general | solution.py:66
  118.5 0.0 all-reduce.3.cloned.1.call-update
  118.5 0.2 all-reduce.5.cloned.1.call-start
  118.8 54.8 %all-reduce.3.cloned.1.call-done = f32[4096,64]{0,1:T(8,128)} async-done(((f32[4096,64]{0,1:T(8,128)}), f32[4096,64]{0,1:T(8,128)}) %all-reduce.3.cloned.1.call-update) | async-done | bytes 1048592 | tf_op jit(solution)/shard_map/psum | solution.py:67
  173.6 2.7 %fusion.5 = f32[64,64]{1,0:T(8,128)S(1)} fusion(f32[4096,64]{0,1:T(8,128)} %all-reduce.3.cloned.1.call-done), kind=kOutput, calls=%fused_computation.11 | convolution fusion | flops 201588736 | bytes 1064960 | tf_op jit(solution)/shard_map/dot_general | solution.py:68
  176.3 0.1 copy.8
  176.4 5.8 %cholesky.16 = f32[64,64]{1,0:T(8,128)S(1)} custom-call(f32[64,64]{1,0:T(8,128)S(1)} %fusion.13), custom_call_target="Cholesky" | custom-call | tf_op jit(solution)/shard_map/jit(cholesky)/cholesky | solution.py:69
  182.3 0.6 compare_reduce_fusion
  182.9 0.7 fusion.11
  183.6 4.9 %custom-call.6 = f32[1,64,64]{1,2,0:T(8,128)S(1)} custom-call(f32[1,64,64]{2,1,0:T(8,128)S(1)} %fusion.11), custom_call_target="InvertDiagBlocksLowerTriangular" | custom-call | tf_op jit(solution)/shard_map/triangular_solve | solution.py:70
  188.5 2.3 fusion.3
  190.8 11.1 %fusion.17 = f32[512,64]{0,1:T(8,128)} fusion(f32[512,4096]{1,0:T(8,128)} %copy-done.2, f32[4096,64]{0,1:T(8,128)S(1)} %fusion.3), kind=kOutput, calls=%fused_computation.31 | convolution fusion | flops 1610612736 | bytes 9568256 | tf_op jit(solution)/shard_map/dv,dr->vr/dot_general | solution.py:71
  201.9 0.0 all-reduce.5.cloned.1.call-update
  202.0 1.1 multiply_bitcast_fusion
  203.0 51.8 %all-reduce.5.cloned.1.call-done = f32[512,64]{0,1:T(8,128)} async-done(((f32[512,64]{0,1:T(8,128)}), f32[512,64]{0,1:T(8,128)}) %all-reduce.5.cloned.1.call-update) | async-done | bytes 131088 | tf_op jit(solution)/shard_map/psum | solution.py:72
  254.8 1.6 multiply_bitcast_fusion.1
  (9 shorter events, 0.3 us)
Async XLA Ops:
  7.2 100.3 %copy-start = (bf16[1,1,2,64,4096]{4,3,2,1,0:T(8,128)(2,1)S(1)}, bf16[1,1,2,64,4096]{4,3,2,1,0:T(8,128)(2,1)}, u32[]{:S(2)}) copy-start(bf16[1,1,2,64,4096]{4,3,2,1,0:T(8,128)(2,1)} %param.10) | copy-start | bytes 3145732
  7.2 166.4 %all-reduce.3.cloned.1.call-start = ((), (), s32[]{:S(2)}) async-start(), calls=%async_computation | async-start | bytes 2097152 | tf_op jit(solution)/shard_map/psum | solution.py:67
  9.6 16.9 %collective-permute-start = (bf16[64,4096]{1,0:T(8,128)(2,1)S(1)}, bf16[64,4096]{1,0:T(8,128)(2,1)S(1)}, u32[]{:S(2)}, u32[]{:S(2)}) collective-permute-start(bf16[64,4096]{1,0:T(8,128)(2,1)S(1)} %get-tuple-element.332), channel_id=1, source_target_pairs={{1,0},{2,1},{3,2},{5,4},{6,5},{7,6},{9,8},{10,9},{11,10},{13,12},{... | collective-permute-start | bytes 1572872 | tf_op jit(solution)/shard_map/while/body/eval_jaxpr/ppermute | solution.py:12
  26.6 15.0 %collective-permute-start = (bf16[64,4096]{1,0:T(8,128)(2,1)S(1)}, bf16[64,4096]{1,0:T(8,128)(2,1)S(1)}, u32[]{:S(2)}, u32[]{:S(2)}) collective-permute-start(bf16[64,4096]{1,0:T(8,128)(2,1)S(1)} %get-tuple-element.332), channel_id=1, source_target_pairs={{1,0},{2,1},{3,2},{5,4},{6,5},{7,6},{9,8},{10,9},{11,10},{13,12},{... | collective-permute-start | bytes 1572872 | tf_op jit(solution)/shard_map/while/body/eval_jaxpr/ppermute | solution.py:12
  41.6 28.7 %collective-permute-start = (bf16[64,4096]{1,0:T(8,128)(2,1)S(1)}, bf16[64,4096]{1,0:T(8,128)(2,1)S(1)}, u32[]{:S(2)}, u32[]{:S(2)}) collective-permute-start(bf16[64,4096]{1,0:T(8,128)(2,1)S(1)} %get-tuple-element.332), channel_id=1, source_target_pairs={{1,0},{2,1},{3,2},{5,4},{6,5},{7,6},{9,8},{10,9},{11,10},{13,12},{... | collective-permute-start | bytes 1572872 | tf_op jit(solution)/shard_map/while/body/eval_jaxpr/ppermute | solution.py:12
  70.3 3.7 %copy-start.1 = (bf16[4096,512]{1,0:T(8,128)(2,1)S(1)}, bf16[4096,512]{1,0:T(8,128)(2,1)}, u32[]{:S(2)}) copy-start(bf16[4096,512]{1,0:T(8,128)(2,1)} %get-tuple-element.246) | copy-start | bytes 12582916 | tf_op jit(solution)/shard_map/while/body/eval_jaxpr/cond
  75.5 13.8 %collective-permute-start = (bf16[64,4096]{1,0:T(8,128)(2,1)S(1)}, bf16[64,4096]{1,0:T(8,128)(2,1)S(1)}, u32[]{:S(2)}, u32[]{:S(2)}) collective-permute-start(bf16[64,4096]{1,0:T(8,128)(2,1)S(1)} %get-tuple-element.332), channel_id=1, source_target_pairs={{1,0},{2,1},{3,2},{5,4},{6,5},{7,6},{9,8},{10,9},{11,10},{13,12},{... | collective-permute-start | bytes 1572872 | tf_op jit(solution)/shard_map/while/body/eval_jaxpr/ppermute | solution.py:12
  89.3 3.7 %copy-start.1 = (bf16[4096,512]{1,0:T(8,128)(2,1)S(1)}, bf16[4096,512]{1,0:T(8,128)(2,1)}, u32[]{:S(2)}) copy-start(bf16[4096,512]{1,0:T(8,128)(2,1)} %get-tuple-element.246) | copy-start | bytes 12582916 | tf_op jit(solution)/shard_map/while/body/eval_jaxpr/cond
  94.4 13.0 %collective-permute-start = (bf16[64,4096]{1,0:T(8,128)(2,1)S(1)}, bf16[64,4096]{1,0:T(8,128)(2,1)S(1)}, u32[]{:S(2)}, u32[]{:S(2)}) collective-permute-start(bf16[64,4096]{1,0:T(8,128)(2,1)S(1)} %get-tuple-element.332), channel_id=1, source_target_pairs={{1,0},{2,1},{3,2},{5,4},{6,5},{7,6},{9,8},{10,9},{11,10},{13,12},{... | collective-permute-start | bytes 1572872 | tf_op jit(solution)/shard_map/while/body/eval_jaxpr/ppermute | solution.py:12
  107.4 4.5 %copy-start.3 = (f32[1,512,64]{1,2,0:T(8,128)S(1)}, f32[1,512,64]{1,2,0:T(8,128)}, u32[]{:S(2)}) copy-start(f32[1,512,64]{1,2,0:T(8,128)} %param.15) | copy-start | bytes 393220
  108.7 3.2 %copy-start.2 = (f32[512,4096]{1,0:T(8,128)}, f32[512,4096]{1,0:T(8,128)S(1)}, u32[]{:S(2)}) copy-start(f32[512,4096]{1,0:T(8,128)S(1)} %fusion.16) | copy-start | bytes 25165828
  118.5 136.3 %all-reduce.5.cloned.1.call-start = ((), (), s32[]{:S(2)}) async-start(), calls=%async_computation.1 | async-start | bytes 262144 | tf_op jit(solution)/shard_map/psum | solution.py:72
Sparse Core Ops, SparseCore 0:
  118.6 54.8 all-reduce.2
  202.1 52.6 all-reduce.4
where the time goes:
time: 264 us; the launch traced here: 263 us
  waiting for transfers between devices  188 us (71%)
  matrix products  34.3 us (13%)
  other arithmetic  16.9 us (6%)
  between operations  14.1 us (5%)
  starting transfers between devices  6.72 us (3%)
  local copies, waits for them, and re-layouts  3.47 us (1%)
    ppermute x5, waiting for transfers between devices, passed_along(): lax.ppermute(value, axis, [(source, source + steps) for source in range(i...  80.9 us
    psum x1, waiting for transfers between devices, local(): left = lax.psum(term_left, 'dp') / replicas  54.8 us
    psum x1, waiting for transfers between devices, local(): fresh = lax.psum(term_right, 'dp') / replicas  51.8 us
    dot_general x1, matrix products, local(): term_right = jnp.einsum('dv,dr->vr', gradient, unit, precision=high)  11.1 us
    dot_general x2, matrix products, propagate(): jnp.einsum('td,vd->tv', grad_in, w_output, preferred_element_type=jnp.flo...  7.46 us
    dot_general x1, matrix products, local(): term_left = jnp.dot(gradient, right, precision=high)  6.58 us
    another operation x3, other arithmetic, local(): lower = jnp.linalg.cholesky(gram)  6.52 us
    ppermute x5, starting transfers between devices, passed_along(): lax.ppermute(value, axis, [(source, source + steps) for source in range(i...  6.46 us
  transfers between devices with their start and end apart: 7, of which 7 were waited for; matrix products, arithmetic and copies ran while one was open for 0% of the time, Pallas kernels for 0%

commit v1 on v0

--- a/solution.py
+++ b/solution.py
@@ -1,9 +1,335 @@
+import functools
 import math
 
 import jax
 import jax.numpy as jnp
 from jax import lax
+from jax.experimental import pallas as pl
+from jax.experimental.pallas import tpu as pltpu
 from jax.sharding import PartitionSpec as P
+
+MESH = pl.DeviceIdType.MESH
+CHUNK = 16
+BLOCK = 4
+F32 = jnp.float32
+BF16 = jnp.bfloat16
+
+
+def dot(a, b, dims):
+    return lax.dot_general(a, b, ((dims[0], dims[1]), ((), ())), preferred_element_type=F32)
+
+
+def halves(value):
+    high = value.astype(BF16)
+    low = (value - high.astype(F32)).astype(BF16)
+    return high, low
+
+
+def paired(value, axis):
+    return jnp.concatenate(halves(value), axis=axis)
+
+
+def folded(both, axis):
+    half = both.shape[axis] // 2
+    if axis == 0:
+        return both[:half] + both[half:]
+    return both[:, :half] + both[:, half:]
+
+
+def inverse_factor(gram):
+    rank = gram.shape[0]
+    row_id = lax.broadcasted_iota(jnp.int32, (rank, rank), 0)
+    col_id = lax.broadcasted_iota(jnp.int32, (rank, rank), 1)
+    eye = (row_id == col_id).astype(F32)
+    full = jnp.concatenate([gram, eye], axis=1)
+    wide_row = lax.broadcasted_iota(jnp.int32, (rank, 2 * rank), 0)
+    for j in range(0, rank, BLOCK):
+        cols = [jnp.broadcast_to(full[:, j + i : j + i + 1], (rank, 2 * rank)) for i in range(BLOCK)]
+        rows = [full[j + i : j + i + 1, :] for i in range(BLOCK)]
+        for i in range(BLOCK):
+            inv = 1.0 / cols[i][j + i : j + i + 1, :]
+            scaled = rows[i] * inv
+            for k in range(i + 1, BLOCK):
+                factor = cols[i][j + k : j + k + 1, :]
+                rows[k] = rows[k] - factor * scaled
+                cols[k] = cols[k] - cols[i] * (factor * inv)
+            full = full - jnp.where(wide_row > j + i, cols[i], 0.0) * scaled
+    pivots = jnp.sum(jnp.where(row_id == col_id, full[:, :rank], 0.0), axis=1, keepdims=True)
+    return full[:, rank:] * (1.0 / jnp.sqrt(pivots))
+
+
+def relay(
+    replicas, sections, acts, wv_hbm, wo_hbm, tg_hbm, mask_hbm, q_hbm, basis, fresh,
+    xall, wv, wo, tg, mask, q, gin, gout, dvall, leftall, gramall, wpart, wparts, wsums,
+    local_sem, x_send, x_recv, g_send, g_recv, dv_send, dv_recv,
+    gram_send, gram_recv, left_send, left_recv, wp_send, wp_recv, ws_send, ws_recv,
+):
+    me = lax.axis_index("dp")
+    here = lax.axis_index("section")
+    at_end = here == sections - 1
+    at_start = here == 0
+    chunks, size, width = gin.shape
+    tokens = chunks * size
+    piece = xall.shape[2]
+    rank, features = q.shape
+    share = rank // replicas
+    batches, batch_tokens = mask.shape
+
+    def peer(step):
+        return lax.rem(me + step, replicas)
+
+    def remote(src, dst, send, recv, target):
+        return pltpu.make_async_remote_copy(
+            src_ref=src, dst_ref=dst, send_sem=send, recv_sem=recv,
+            device_id=target, device_id_type=MESH,
+        )
+
+    load_wo = pltpu.make_async_copy(wo_hbm, wo, local_sem.at[0])
+    load_wv = pltpu.make_async_copy(wv_hbm, wv, local_sem.at[1])
+    load_tg = pltpu.make_async_copy(tg_hbm, tg, local_sem.at[2])
+    load_mask = pltpu.make_async_copy(mask_hbm, mask, local_sem.at[3])
+    load_q = pltpu.make_async_copy(q_hbm, q, local_sem.at[4])
+    own_cols = pl.ds(pl.multiple_of(me * piece, piece), piece)
+    load_x = pltpu.make_async_copy(acts.at[:, own_cols], xall.at[me], local_sem.at[5])
+
+    @pl.when(at_end)
+    def _():
+        load_mask.start()
+        load_tg.start()
+
+    load_wo.start()
+    load_wv.start()
+    load_q.start()
+    load_x.start()
+
+    barrier = pltpu.get_barrier_semaphore()
+    for step in range(1, replicas):
+        pl.semaphore_signal(barrier, inc=1, device_id=(peer(step), here), device_id_type=MESH)
+
+    @pl.when(jnp.logical_not(at_start))
+    def _():
+        pl.semaphore_signal(barrier, inc=1, device_id=(me, here - 1), device_id_type=MESH)
+
+    @pl.when(jnp.logical_not(at_end))
+    def _():
+        pl.semaphore_signal(barrier, inc=1, device_id=(me, here + 1), device_id_type=MESH)
+
+    beside = jnp.where(at_start, 0, 1) + jnp.where(at_end, 0, 1)
+    pl.semaphore_wait(barrier, replicas - 1 + beside)
+
+    def x_copy(step):
+        to = peer(step)
+        cols = pl.ds(pl.multiple_of(to * piece, piece), piece)
+        return remote(acts.at[:, cols], xall.at[me], x_send.at[step], x_recv.at[me], (to, here))
+
+    for step in range(1, replicas):
+        x_copy(step).start()
+
+    @pl.when(at_end)
+    def _():
+        load_mask.wait()
+        load_tg.wait()
+        diagonal = lax.broadcasted_iota(jnp.int32, (batch_tokens, batch_tokens), 0) == lax.broadcasted_iota(
+            jnp.int32, (batch_tokens, batch_tokens), 1
+        )
+        per = batch_tokens // size
+        for batch in range(batches):
+            line = mask[batch : batch + 1, :].astype(F32)
+            column = jnp.sum(jnp.where(diagonal, line, 0.0), axis=1, keepdims=True)
+            for part in range(per):
+                at = batch * per + part
+                gin[at] = (tg[at].astype(F32) * column[part * size : (part + 1) * size]).astype(BF16)
+
+    load_wo.wait()
+
+    def g_copy(c):
+        return remote(gout.at[c], gin.at[c], g_send.at[c], g_recv.at[c], (me, here - 1))
+
+    def dv_copy(c, step):
+        return remote(
+            dvall.at[me, c], dvall.at[me, c], dv_send.at[step, c], dv_recv.at[me, c], (peer(step), here)
+        )
+
+    load_wv.wait()
+
+    def advance(c, carry):
+        @pl.when(jnp.logical_not(at_end))
+        def _():
+            remote(gin.at[c], gin.at[c], g_send.at[c], g_recv.at[c], (me, here + 1)).wait_recv()
+
+        grad = gin[c]
+        dvalue = dot(grad, wo[...], ((1,), (1,))).astype(BF16)
+        dvall[me, c] = dvalue
+
+        @pl.when(jnp.logical_not(at_start))
+        def _():
+            gout[c] = (grad.astype(F32) + dot(dvalue, wv[...], ((1,), (1,)))).astype(BF16)
+            g_copy(c).start()
+
+        for step in range(1, replicas):
+            dv_copy(c, step).start()
+        return carry
+
+    lax.fori_loop(0, chunks, advance, 0)
+
+    load_x.wait()
+    load_q.wait()
+    for step in range(1, replicas):
+        other = peer(step)
+        remote(xall.at[other], xall.at[other], x_send.at[step], x_recv.at[other], (other, here)).wait_recv()
+
+    def dv_arrived(c, carry):
+        for step in range(1, replicas):
+            other = peer(step)
+            remote(
+                dvall.at[other, c], dvall.at[other, c], dv_send.at[step, c], dv_recv.at[other, c], (other, here)
+            ).wait_recv()
+        return carry
+
+    lax.fori_loop(0, chunks, dv_arrived, 0)
+
+    everything = xall[...].reshape(replicas * tokens, piece)
+    dvalues = dvall[...].reshape(replicas * tokens, features)
+    base = folded(dot(dvalues, paired(q[...], 0), ((1,), (1,))), 1)
+    left = folded(dot(paired(base, 1), everything, ((0,), (0,))), 0) * (1.0 / replicas)
+    gramall[me] = lax.dot_general(
+        left, left, (((1,), (1,)), ((), ())), precision=lax.Precision.HIGHEST, preferred_element_type=F32
+    )
+
+    def gram_copy(step):
+        return remote(gramall.at[me], gramall.at[me], gram_send.at[step], gram_recv.at[me], (peer(step), here))
+
+    for step in range(1, replicas):
+        gram_copy(step).start()
+    leftall[me] = left.astype(BF16)
+
+    def left_copy(step):
+        return remote(leftall.at[me], leftall.at[me], left_send.at[step], left_recv.at[me], (peer(step), here))
+
+    response = folded(dot(everything, paired(left, 0), ((1,), (1,))), 1)
+    wpart[...] = folded(dot(paired(response, 1), dvalues, ((0,), (0,))), 0).reshape(replicas, share, features)
+
+    def wp_copy(step):
+        to = peer(step)
+        return remote(wpart.at[to], wparts.at[me], wp_send.at[step], wp_recv.at[me], (to, here))
+
+    for step in range(1, replicas):
+        wp_copy(step).start()
+    for step in range(1, replicas):
+        left_copy(step).start()
+    wparts[me] = wpart[me]
+
+    for step in range(1, replicas):
+        other = peer(step)
+        remote(gramall.at[other], gramall.at[other], gram_send.at[step], gram_recv.at[other], (other, here)).wait_recv()
+    for step in range(1, replicas):
+        other = peer(step)
+        remote(wparts.at[other], wparts.at[other], wp_send.at[step], wp_recv.at[other], (other, here)).wait_recv()
+    total = wparts[0]
+    for index in range(1, replicas):
+        total = total + wparts[index]
+    wsums[me] = total * (1.0 / replicas)
+
+    def ws_copy(step):
+        return remote(wsums.at[me], wsums.at[me], ws_send.at[step], ws_recv.at[me], (peer(step), here))
+
+    for step in range(1, replicas):
+        ws_copy(step).start()
+
+    gram = gramall[0]
+    for index in range(1, replicas):
+        gram = gram + gramall[index]
+    inverse = inverse_factor(gram)
+    factors = paired(inverse, 0)
+
+    for step in range(1, replicas):
+        other = peer(step)
+        remote(leftall.at[other], leftall.at[other], left_send.at[step], left_recv.at[other], (other, here)).wait_recv()
+    scale = math.sqrt(width)
+    for index in range(replicas):
+        basis[:, index * piece : (index + 1) * piece] = (
+            folded(dot(factors, leftall[index], ((1,), (0,))), 0) * scale
+        )
+
+    for step in range(1, replicas):
+        other = peer(step)
+        remote(wsums.at[other], wsums.at[other], ws_send.at[step], ws_recv.at[other], (other, here)).wait_recv()
+    fresh[...] = lax.dot_general(
+        inverse, wsums[...].reshape(rank, features), (((1,), (0,)), ((), ())),
+        precision=lax.Precision.HIGHEST, preferred_element_type=F32,
+    )
+
+    for step in range(1, replicas):
+        x_copy(step).wait_send()
+        gram_copy(step).wait_send()
+        wp_copy(step).wait_send()
+        left_copy(step).wait_send()
+        ws_copy(step).wait_send()
+
+    def sent(c, carry):
+        for step in range(1, replicas):
+            dv_copy(c, step).wait_send()
+
+        @pl.when(jnp.logical_not(at_start))
+        def _():
+            g_copy(c).wait_send()
+
+        return carry
+
+    lax.fori_loop(0, chunks, sent, 0)
+
+
+def local_kernel(replicas, sections, acts, weight_v, weight_o, top_grad, loss_mask, q_prev):
+    _, _, batches, batch_tokens, width = acts.shape
+    tokens = batches * batch_tokens
+    _, features, rank = q_prev.shape
+    size = CHUNK
+    chunks = tokens // size
+    piece = width // replicas
+    share = rank // replicas
+    any_spec = pl.BlockSpec(memory_space=pl.ANY)
+    vmem = pl.BlockSpec(memory_space=pltpu.VMEM)
+    dma = pltpu.SemaphoreType.DMA
+    basis, fresh = pl.pallas_call(
+        functools.partial(relay, replicas, sections),
+        out_shape=(
+            jax.ShapeDtypeStruct((rank, width), F32),
+            jax.ShapeDtypeStruct((rank, features), F32),
+        ),
+        in_specs=[any_spec] * 6,
+        out_specs=(vmem, vmem),
+        scratch_shapes=[
+            pltpu.VMEM((replicas, tokens, piece), BF16),
+            pltpu.VMEM((width, features), BF16),
+            pltpu.VMEM((features, width), BF16),
+            pltpu.VMEM((chunks, size, width), BF16),
+            pltpu.VMEM((batches, batch_tokens), jnp.int32),
+            pltpu.VMEM((rank, features), F32),
+            pltpu.VMEM((chunks, size, width), BF16),
+            pltpu.VMEM((chunks, size, width), BF16),
+            pltpu.VMEM((replicas, chunks, size, features), BF16),
+            pltpu.VMEM((replicas, rank, piece), BF16),
+            pltpu.VMEM((replicas, rank, rank), F32),
+            pltpu.VMEM((replicas, share, features), F32),
+            pltpu.VMEM((replicas, share, features), F32),
+            pltpu.VMEM((replicas, share, features), F32),
+            dma((6,)),
+            dma((replicas,)), dma((replicas,)),
+            dma((chunks,)), dma((chunks,)),
+            dma((replicas, chunks)), dma((replicas, chunks)),
+            dma((replicas,)), dma((replicas,)),
+            dma((replicas,)), dma((replicas,)),
+            dma((replicas,)), dma((replicas,)),
+            dma((replicas,)), dma((replicas,)),
+        ],
+        compiler_params=pltpu.CompilerParams(
+            collective_id=0, has_side_effects=True, vmem_limit_bytes=60 * 1024 * 1024
+        ),
+    )(
+        acts.reshape(tokens, width), weight_v[0], weight_o[0],
+        top_grad.reshape(chunks, size, width), loss_mask[0], q_prev[0].T,
+    )
+    return (basis.T[None], fresh.T[None])
 
 
 def passed_along(value, axis, steps):
@@ -82,8 +408,25 @@
         P("dp", None, None),
         P("section", None, None),
     )
+    replicas = mesh.shape["dp"]
+    sections = mesh.shape["section"]
+
+    def body(acts, weight_v, weight_o, top_grad, loss_mask, q_prev):
+        args = (acts, weight_v, weight_o, top_grad, loss_mask, q_prev)
+        width, features = weight_v.shape[1:]
+        fits = (
+            replicas > 1
+            and width % (replicas * 128) == 0
+            and q_prev.shape[2] % (replicas * 8) == 0
+            and acts.shape[3] % CHUNK == 0
+            and q_prev.shape[2] % BLOCK == 0
+        )
+        if fits:
+            return local_kernel(replicas, sections, *args)
+        return local(*args)
+
     return jax.shard_map(
-        local,
+        body,
         mesh=mesh,
         in_specs=placed,
         out_specs=(P("section", None, None), P("section", None, None)),

time: 264 us -> 74.6 us (0.28)
  waiting for transfers between devices: 188 us -> 0 us
  Pallas kernels: 0 us -> 69.9 us
  matrix products: 34.3 us -> 0 us
  other arithmetic: 16.9 us -> 0 us
  between operations: 14.1 us -> 0.64 us
  starting transfers between devices: 6.72 us -> 0 us
    psum x2 -> x0, waiting for transfers between devices: 107 us -> none  [the longest x1 54.8 us: local(): left = lax.psum(term_left, 'dp') / replicas]
    ppermute x5 -> x0, waiting for transfers between devices: 80.9 us -> none  [passed_along(): lax.ppermute(value, axis, [(source, source + steps) for source in range(i...]
    pallas_call x0 -> x1, Pallas kernels: none -> 69.9 us  [local_kernel(): pl.pallas_call(functools.partial(relay, replicas, sections), out_shape=(j...]
    dot_general x8 -> x0, matrix products: 31.9 us -> none  [the longest x1 11.1 us: local(): term_right = jnp.einsum('dv,dr->vr', gradient, unit, precision=high)]
    another operation x5 -> x0, other arithmetic: 12.1 us -> none  [the longest x3 6.52 us: local(): lower = jnp.linalg.cholesky(gram)]
    ppermute x5 -> x0, starting transfers between devices: 6.46 us -> none  [passed_along(): lax.ppermute(value, axis, [(source, source + steps) for source in range(i...]
  transfers between devices with their start and end apart: 7 -> 0, of which waited for: 7 -> 0; matrix products, arithmetic and copies ran while one was open for 0% -> 0% of each run, Pallas kernels for 0% -> 0%
where the time goes in v1:
time: 74.6 us; the launch traced here: 74.4 us
  Pallas kernels  69.9 us (94%)
  local copies, waits for them, and re-layouts  3.84 us (5%)
    pallas_call x1, Pallas kernels, local_kernel(): pl.pallas_call(functools.partial(relay, replicas, sections), out_shape=(j...  69.9 us
    unnamed x2, local copies, waits for them, and re-layouts  3.84 us

profile of v1, /device:TPU:0, one launch (start us, length us, event | category | flops | bytes accessed | tf_op | source)
XLA Modules:
  0.0 74.4 jit_solution(12379679088706832799)
XLA Ops:
  0.6 69.9 %shard_map.77 = (f32[64,4096]{1,0:T(8,128)}, f32[64,512]{1,0:T(8,128)}) custom-call(bf16[128,4096]{1,0:T(8,128)(2,1)} %bitcast.17, bf16[4096,512]{1,0:T(8,128)(2,1)} %bitcast.14, bf16[512,4096]{1,0:T(8,128)(2,1)} %bitcast.15, bf16[8,16,4096]{2,1,0:T(8,128)(2,1)} %bitcast.18, s32[2,64]{1,0:T(2,128)} %bitcast.21, f32[64,512]{1,0:T(8,128)} %bitcast.19), custom_call_target="tpu_custom_call" | custom-call | tf_op jit(solution)/shard_map/pallas_call | solution.py:293
  70.6 2.3 %copy.10 = f32[1,4096,64]{1,2,0:T(8,128)} copy(f32[1,4096,64]{1,2,0:T(8,128)} %bitcast.16) | data formatting | bytes 2097152
  72.8 1.6 %copy.11 = f32[1,512,64]{1,2,0:T(8,128)} copy(f32[1,512,64]{1,2,0:T(8,128)} %bitcast.20) | data formatting | bytes 262144

commit v2 on v1

--- a/solution.py
+++ b/solution.py
@@ -11,6 +11,7 @@
 MESH = pl.DeviceIdType.MESH
 CHUNK = 16
 BLOCK = 4
+PARTS = 4
 F32 = jnp.float32
 BF16 = jnp.bfloat16
 
@@ -59,9 +60,9 @@
 
 
 def relay(
-    replicas, sections, acts, wv_hbm, wo_hbm, tg_hbm, mask_hbm, q_hbm, basis, fresh,
-    xall, wv, wo, tg, mask, q, gin, gout, dvall, leftall, gramall, wpart, wparts, wsums,
-    local_sem, x_send, x_recv, g_send, g_recv, dv_send, dv_recv,
+    replicas, sections, acts, wv_hbm, wo_hbm, tg_hbm, mask_hbm, q_hbm, leftall, wsums, inverse_out,
+    xall, wv, wo, tg, mask, q, gin, gout, dvall, gramall, wpart, wparts,
+    local_sem, wo_sem, wv_sem, x_send, x_recv, g_send, g_recv, dv_send, dv_recv,
     gram_send, gram_recv, left_send, left_recv, wp_send, wp_recv, ws_send, ws_recv,
 ):
     me = lax.axis_index("dp")
@@ -84,8 +85,16 @@
             device_id=target, device_id_type=MESH,
         )
 
-    load_wo = pltpu.make_async_copy(wo_hbm, wo, local_sem.at[0])
-    load_wv = pltpu.make_async_copy(wv_hbm, wv, local_sem.at[1])
+    column = width // PARTS
+
+    def load_wo(part):
+        cols = pl.ds(part * column, column)
+        return pltpu.make_async_copy(wo_hbm.at[:, cols], wo.at[:, cols], wo_sem.at[part])
+
+    def load_wv(part):
+        cols = pl.ds(part * column, column)
+        return pltpu.make_async_copy(wv_hbm.at[cols], wv.at[cols], wv_sem.at[part])
+
     load_tg = pltpu.make_async_copy(tg_hbm, tg, local_sem.at[2])
     load_mask = pltpu.make_async_copy(mask_hbm, mask, local_sem.at[3])
     load_q = pltpu.make_async_copy(q_hbm, q, local_sem.at[4])
@@ -97,8 +106,10 @@
         load_mask.start()
         load_tg.start()
 
-    load_wo.start()
-    load_wv.start()
+    for part in range(PARTS):
+        load_wo(part).start()
+    for part in range(PARTS):
+        load_wv(part).start()
     load_q.start()
     load_x.start()
 
@@ -113,17 +124,11 @@
     @pl.when(jnp.logical_not(at_end))
     def _():
         pl.semaphore_signal(barrier, inc=1, device_id=(me, here + 1), device_id_type=MESH)
-
-    beside = jnp.where(at_start, 0, 1) + jnp.where(at_end, 0, 1)
-    pl.semaphore_wait(barrier, replicas - 1 + beside)
 
     def x_copy(step):
         to = peer(step)
         cols = pl.ds(pl.multiple_of(to * piece, piece), piece)
         return remote(acts.at[:, cols], xall.at[me], x_send.at[step], x_recv.at[me], (to, here))
-
-    for step in range(1, replicas):
-        x_copy(step).start()
 
     @pl.when(at_end)
     def _():
@@ -135,36 +140,62 @@
         per = batch_tokens // size
         for batch in range(batches):
             line = mask[batch : batch + 1, :].astype(F32)
-            column = jnp.sum(jnp.where(diagonal, line, 0.0), axis=1, keepdims=True)
+            keep = jnp.sum(jnp.where(diagonal, line, 0.0), axis=1, keepdims=True)
             for part in range(per):
                 at = batch * per + part
-                gin[at] = (tg[at].astype(F32) * column[part * size : (part + 1) * size]).astype(BF16)
-
-    load_wo.wait()
-
-    def g_copy(c):
-        return remote(gout.at[c], gin.at[c], g_send.at[c], g_recv.at[c], (me, here - 1))
+                gin[at] = (tg[at].astype(F32) * keep[part * size : (part + 1) * size]).astype(BF16)
+
+    beside = jnp.where(at_start, 0, 1) + jnp.where(at_end, 0, 1)
+    pl.semaphore_wait(barrier, replicas - 1 + beside)
+
+    for step in range(1, replicas):
+        x_copy(step).start()
+
+    def g_copy(c, part):
+        cols = pl.ds(part * column, column)
+        return remote(
+            gout.at[c, :, cols], gin.at[c, :, cols], g_send.at[c, part], g_recv.at[c, part], (me, here - 1)
+        )
 
     def dv_copy(c, step):
         return remote(
             dvall.at[me, c], dvall.at[me, c], dv_send.at[step, c], dv_recv.at[me, c], (peer(step), here)
         )
 
-    load_wv.wait()
-
     def advance(c, carry):
-        @pl.when(jnp.logical_not(at_end))
-        def _():
-            remote(gin.at[c], gin.at[c], g_send.at[c], g_recv.at[c], (me, here + 1)).wait_recv()
-
-        grad = gin[c]
-        dvalue = dot(grad, wo[...], ((1,), (1,))).astype(BF16)
+        total = None
+        for part in range(PARTS):
+            cols = slice(part * column, (part + 1) * column)
+            spot = pl.ds(part * column, column)
+
+            @pl.when(c == 0)
+            def _():
+                load_wo(part).wait()
+
+            @pl.when(jnp.logical_not(at_end))
+            def _():
+                remote(
+                    gin.at[c, :, spot], gin.at[c, :, spot], g_send.at[c, part], g_recv.at[c, part], (me, here + 1)
+                ).wait_recv()
+
+            term = dot(gin[c, :, cols], wo[:, cols], ((1,), (1,)))
+            total = term if part == 0 else total + term
+        dvalue = total.astype(BF16)
         dvall[me, c] = dvalue
 
-        @pl.when(jnp.logical_not(at_start))
-        def _():
-            gout[c] = (grad.astype(F32) + dot(dvalue, wv[...], ((1,), (1,)))).astype(BF16)
-            g_copy(c).start()
+        for part in range(PARTS):
+            cols = slice(part * column, (part + 1) * column)
+
+            @pl.when(c == 0)
+            def _():
+                load_wv(part).wait()
+
+            @pl.when(jnp.logical_not(at_start))
+            def _():
+                gout[c, :, cols] = (
+                    gin[c, :, cols].astype(F32) + dot(dvalue, wv[cols, :], ((1,), (1,)))
+                ).astype(BF16)
+                g_copy(c, part).start()
 
         for step in range(1, replicas):
             dv_copy(c, step).start()
@@ -192,20 +223,20 @@
     dvalues = dvall[...].reshape(replicas * tokens, features)
     base = folded(dot(dvalues, paired(q[...], 0), ((1,), (1,))), 1)
     left = folded(dot(paired(base, 1), everything, ((0,), (0,))), 0) * (1.0 / replicas)
+    def gram_copy(step):
+        return remote(gramall.at[me], gramall.at[me], gram_send.at[step], gram_recv.at[me], (peer(step), here))
+
+    def left_copy(step):
+        return remote(leftall.at[me], leftall.at[me], left_send.at[step], left_recv.at[me], (peer(step), here))
+
+    leftall[me] = left.astype(BF16)
     gramall[me] = lax.dot_general(
         left, left, (((1,), (1,)), ((), ())), precision=lax.Precision.HIGHEST, preferred_element_type=F32
     )
-
-    def gram_copy(step):
-        return remote(gramall.at[me], gramall.at[me], gram_send.at[step], gram_recv.at[me], (peer(step), here))
-
     for step in range(1, replicas):
         gram_copy(step).start()
-    leftall[me] = left.astype(BF16)
-
-    def left_copy(step):
-        return remote(leftall.at[me], leftall.at[me], left_send.at[step], left_recv.at[me], (peer(step), here))
-
+    for step in range(1, replicas):
+        left_copy(step).start()
     response = folded(dot(everything, paired(left, 0), ((1,), (1,))), 1)
     wpart[...] = folded(dot(paired(response, 1), dvalues, ((0,), (0,))), 0).reshape(replicas, share, features)
 
@@ -215,8 +246,6 @@
 
     for step in range(1, replicas):
         wp_copy(step).start()
-    for step in range(1, replicas):
-        left_copy(step).start()
     wparts[me] = wpart[me]
 
     for step in range(1, replicas):
@@ -240,25 +269,14 @@
     for index in range(1, replicas):
         gram = gram + gramall[index]
     inverse = inverse_factor(gram)
-    factors = paired(inverse, 0)
+    inverse_out[...] = inverse
 
     for step in range(1, replicas):
         other = peer(step)
         remote(leftall.at[other], leftall.at[other], left_send.at[step], left_recv.at[other], (other, here)).wait_recv()
-    scale = math.sqrt(width)
-    for index in range(replicas):
-        basis[:, index * piece : (index + 1) * piece] = (
-            folded(dot(factors, leftall[index], ((1,), (0,))), 0) * scale
-        )
-
     for step in range(1, replicas):
         other = peer(step)
         remote(wsums.at[other], wsums.at[other], ws_send.at[step], ws_recv.at[other], (other, here)).wait_recv()
-    fresh[...] = lax.dot_general(
-        inverse, wsums[...].reshape(rank, features), (((1,), (0,)), ((), ())),
-        precision=lax.Precision.HIGHEST, preferred_element_type=F32,
-    )
-
     for step in range(1, replicas):
         x_copy(step).wait_send()
         gram_copy(step).wait_send()
@@ -272,11 +290,26 @@
 
         @pl.when(jnp.logical_not(at_start))
         def _():
-            g_copy(c).wait_send()
+            for part in range(PARTS):
+                g_copy(c, part).wait_send()
 
         return carry
 
     lax.fori_loop(0, chunks, sent, 0)
+
+
+def finish(leftall, wsums, inverse, basis, fresh):
+    replicas, rank, piece = leftall.shape
+    factors = paired(inverse[...], 0)
+    scale = math.sqrt(replicas * piece)
+    for index in range(replicas):
+        basis[:, index * piece : (index + 1) * piece] = (
+            folded(dot(factors, leftall[index], ((1,), (0,))), 0) * scale
+        )
+    fresh[...] = lax.dot_general(
+        inverse[...], wsums[...].reshape(rank, -1), (((1,), (0,)), ((), ())),
+        precision=lax.Precision.HIGHEST, preferred_element_type=F32,
+    )
 
 
 def local_kernel(replicas, sections, acts, weight_v, weight_o, top_grad, loss_mask, q_prev):
@@ -290,14 +323,15 @@
     any_spec = pl.BlockSpec(memory_space=pl.ANY)
     vmem = pl.BlockSpec(memory_space=pltpu.VMEM)
     dma = pltpu.SemaphoreType.DMA
-    basis, fresh = pl.pallas_call(
+    leftall, wsums, inverse = pl.pallas_call(
         functools.partial(relay, replicas, sections),
         out_shape=(
-            jax.ShapeDtypeStruct((rank, width), F32),
-            jax.ShapeDtypeStruct((rank, features), F32),
+            jax.ShapeDtypeStruct((replicas, rank, piece), BF16),
+            jax.ShapeDtypeStruct((replicas, share, features), F32),
+            jax.ShapeDtypeStruct((rank, rank), F32),
         ),
         in_specs=[any_spec] * 6,
-        out_specs=(vmem, vmem),
+        out_specs=(vmem, vmem, vmem),
         scratch_shapes=[
             pltpu.VMEM((replicas, tokens, piece), BF16),
             pltpu.VMEM((width, features), BF16),
@@ -308,14 +342,12 @@
             pltpu.VMEM((chunks, size, width), BF16),
             pltpu.VMEM((chunks, size, width), BF16),
             pltpu.VMEM((replicas, chunks, size, features), BF16),
-            pltpu.VMEM((replicas, rank, piece), BF16),
             pltpu.VMEM((replicas, rank, rank), F32),
             pltpu.VMEM((replicas, share, features), F32),
             pltpu.VMEM((replicas, share, features), F32),
-            pltpu.VMEM((replicas, share, features), F32),
-            dma((6,)),
+            dma((6,)), dma((PARTS,)), dma((PARTS,)),
             dma((replicas,)), dma((replicas,)),
-            dma((chunks,)), dma((chunks,)),
+            dma((chunks, PARTS)), dma((chunks, PARTS)),
             dma((replicas, chunks)), dma((replicas, chunks)),
             dma((replicas,)), dma((replicas,)),
             dma((replicas,)), dma((replicas,)),
@@ -329,6 +361,15 @@
         acts.reshape(tokens, width), weight_v[0], weight_o[0],
         top_grad.reshape(chunks, size, width), loss_mask[0], q_prev[0].T,
     )
+    basis, fresh = pl.pallas_call(
+        finish,
+        out_shape=(
+            jax.ShapeDtypeStruct((rank, width), F32),
+            jax.ShapeDtypeStruct((rank, features), F32),
+        ),
+        in_specs=[vmem] * 3,
+        out_specs=(vmem, vmem),
+    )(leftall, wsums, inverse)
     return (basis.T[None], fresh.T[None])
 
 
@@ -417,6 +458,7 @@
         fits = (
             replicas > 1
             and width % (replicas * 128) == 0
+            and width % (PARTS * 128) == 0
             and q_prev.shape[2] % (replicas * 8) == 0
             and acts.shape[3] % CHUNK == 0
             and q_prev.shape[2] % BLOCK == 0

time: 74.6 us -> 70.9 us (0.950)
  local copies, waits for them, and re-layouts: 3.84 us -> 0 us
    unnamed x2 -> x0, local copies, waits for them, and re-layouts: 3.84 us -> none
    pallas_call x0 -> x1, Pallas kernels: none -> 2.53 us  [local_kernel(): pl.pallas_call(finish, out_shape=(jax.ShapeDtypeStruct((rank, width), F32...]
    pallas_call x1, Pallas kernels: 69.9 us -> 67.5 us  [local_kernel(): pl.pallas_call(functools.partial(relay, replicas, sections), out_shape=(j...]
where the time goes in v2:
time: 70.9 us; the launch traced here: 70.7 us
  Pallas kernels  70.1 us (99%)
    pallas_call x1, Pallas kernels, local_kernel(): pl.pallas_call(functools.partial(relay, replicas, sections), out_shape=(j...  67.5 us
    pallas_call x1, Pallas kernels, local_kernel(): pl.pallas_call(finish, out_shape=(jax.ShapeDtypeStruct((rank, width), F32...  2.53 us

profile of v2, /device:TPU:0, one launch (start us, length us, event | category | flops | bytes accessed | tf_op | source)
XLA Modules:
  0.0 70.7 jit_solution(7658535394225720410)
XLA Ops:
  0.6 67.5 %shard_map.77 = (bf16[8,64,512]{2,1,0:T(8,128)(2,1)}, f32[8,8,512]{2,1,0:T(8,128)}, f32[64,64]{1,0:T(8,128)}) custom-call(bf16[128,4096]{1,0:T(8,128)(2,1)} %bitcast.16, bf16[4096,512]{1,0:T(8,128)(2,1)} %bitcast.14, bf16[512,4096]{1,0:T(8,128)(2,1)} %bitcast.15, bf16[8,16,4096]{2,1,0:T(8,128)(2,1)} %bitcast.17, s32[2,64]{1,0:T(2,128)} %bitcast.19, ...), custom_call_target="tpu_custom_call" | custom-call | tf_op jit(solution)/shard_map/pallas_call | solution.py:326
  68.2 2.5 %shard_map.78 = (f32[64,4096]{1,0:T(8,128)}, f32[64,512]{1,0:T(8,128)}) custom-call(bf16[8,64,512]{2,1,0:T(8,128)(2,1)} %get-tuple-element.7.leftall, f32[8,8,512]{2,1,0:T(8,128)} %get-tuple-element.8.wsums, f32[64,64]{1,0:T(8,128)} %get-tuple-element.9.inverse), custom_call_target="tpu_custom_call" | custom-call | tf_op jit(solution)/shard_map/pallas_call | solution.py:364

commit v3 on v2

--- a/solution.py
+++ b/solution.py
@@ -12,6 +12,7 @@
 CHUNK = 16
 BLOCK = 4
 PARTS = 4
+GROUPS = 2
 F32 = jnp.float32
 BF16 = jnp.bfloat16
 
@@ -162,36 +163,34 @@
             dvall.at[me, c], dvall.at[me, c], dv_send.at[step, c], dv_recv.at[me, c], (peer(step), here)
         )
 
+    for part in range(PARTS):
+        load_wo(part).wait()
+        load_wv(part).wait()
+
     def advance(c, carry):
         total = None
-        for part in range(PARTS):
-            cols = slice(part * column, (part + 1) * column)
-            spot = pl.ds(part * column, column)
-
-            @pl.when(c == 0)
-            def _():
-                load_wo(part).wait()
+        for group in range(GROUPS):
+            per_group = PARTS // GROUPS
 
             @pl.when(jnp.logical_not(at_end))
             def _():
-                remote(
-                    gin.at[c, :, spot], gin.at[c, :, spot], g_send.at[c, part], g_recv.at[c, part], (me, here + 1)
-                ).wait_recv()
-
+                for part in range(group * per_group, (group + 1) * per_group):
+                    spot = pl.ds(part * column, column)
+                    remote(
+                        gin.at[c, :, spot], gin.at[c, :, spot], g_send.at[c, part], g_recv.at[c, part],
+                        (me, here + 1),
+                    ).wait_recv()
+
+            cols = slice(group * per_group * column, (group + 1) * per_group * column)
             term = dot(gin[c, :, cols], wo[:, cols], ((1,), (1,)))
-            total = term if part == 0 else total + term
+            total = term if group == 0 else total + term
         dvalue = total.astype(BF16)
         dvall[me, c] = dvalue
 
-        for part in range(PARTS):
-            cols = slice(part * column, (part + 1) * column)
-
-            @pl.when(c == 0)
-            def _():
-                load_wv(part).wait()
-
-            @pl.when(jnp.logical_not(at_start))
-            def _():
+        @pl.when(jnp.logical_not(at_start))
+        def _():
+            for part in range(PARTS):
+                cols = slice(part * column, (part + 1) * column)
                 gout[c, :, cols] = (
                     gin[c, :, cols].astype(F32) + dot(dvalue, wv[cols, :], ((1,), (1,)))
                 ).astype(BF16)

time: 70.9 us -> 74.7 us (1.054)
  Pallas kernels: 70.1 us -> 73.9 us
    pallas_call x1, Pallas kernels: 67.5 us -> 71.4 us  [local_kernel(): pl.pallas_call(functools.partial(relay, replicas, sections), out_shape=(j...]
where the time goes in v3:
time: 74.7 us; the launch traced here: 74.6 us
  Pallas kernels  73.9 us (99%)
    pallas_call x1, Pallas kernels, local_kernel(): pl.pallas_call(functools.partial(relay, replicas, sections), out_shape=(j...  71.4 us
    pallas_call x1, Pallas kernels, local_kernel(): pl.pallas_call(finish, out_shape=(jax.ShapeDtypeStruct((rank, width), F32...  2.53 us

profile of v3, /device:TPU:0, one launch (start us, length us, event | category | flops | bytes accessed | tf_op | source)
XLA Modules:
  0.0 74.6 jit_solution(7947888138804694151)
XLA Ops:
  0.6 71.4 %shard_map.77 = (bf16[8,64,512]{2,1,0:T(8,128)(2,1)}, f32[8,8,512]{2,1,0:T(8,128)}, f32[64,64]{1,0:T(8,128)}) custom-call(bf16[128,4096]{1,0:T(8,128)(2,1)} %bitcast.16, bf16[4096,512]{1,0:T(8,128)(2,1)} %bitcast.14, bf16[512,4096]{1,0:T(8,128)(2,1)} %bitcast.15, bf16[8,16,4096]{2,1,0:T(8,128)(2,1)} %bitcast.17, s32[2,64]{1,0:T(2,128)} %bitcast.19, ...), custom_call_target="tpu_custom_call" | custom-call | tf_op jit(solution)/shard_map/pallas_call | solution.py:325
  72.0 2.5 %shard_map.78 = (f32[64,4096]{1,0:T(8,128)}, f32[64,512]{1,0:T(8,128)}) custom-call(bf16[8,64,512]{2,1,0:T(8,128)(2,1)} %get-tuple-element.7.leftall, f32[8,8,512]{2,1,0:T(8,128)} %get-tuple-element.8.wsums, f32[64,64]{1,0:T(8,128)} %get-tuple-element.9.inverse), custom_call_target="tpu_custom_call" | custom-call | tf_op jit(solution)/shard_map/pallas_call | solution.py:363
